TPU v7x, 512 devices: a whole 4x4x16 slice. The times are simulated.
512 devices in a mesh: gz: 128 (over z, y, core), row: 4 (over x).
Axes of the slice: x: 4, y: 4, z: 16, core: 2. Of those that a mesh axis runs over, the one named last changes fastest.
Arguments:
- tokens: bfloat16 [262144, 384], P(('gz', 'row')), may hold values from -6 to 6
- key_blocks: int32 [4096, 20], P(('gz', 'row')), may hold values from 0 to 4095, as said below
- counts: int32 [128], replicated, may hold values from 8 to 32, as said below
- norm_gain: float32 [384], replicated, may hold values from 0.1 to 1.9
- qkv_weight: bfloat16 [384, 1152], replicated, may hold values from -1 to 1
- out_weight: bfloat16 [384, 384], replicated, may hold values from -0.3125 to 0.3125
- mlp_gain: float32 [384], replicated, may hold values from 0.1 to 1.9
- up_weight: bfloat16 [384, 1536], replicated, may hold values from -0.3125 to 0.3125
- down_weight: bfloat16 [1536, 384], replicated, may hold values from -0.15625 to 0.15625
Outputs:
- block_out: bfloat16 [262144, 384], P(('gz', 'row'))
Inputs may be any that keep to these rules, and one draw needn't show every extreme that they name: `key_blocks`: entries 0 to 3 of a query block's list name live blocks of the query's own slab (repeats possible). The other 16 entries name blocks with the same row group as the query block (id % 32 // 8 equal), in any slab; over the blocks of one device each slab is named by exactly 1 such entries. `counts`: one slab is full in every draw.
All inputs are finite; a program needn't handle non-finite values.
Results may differ from a plain program's by a relative error of at most 0.01.
Values may be sent and summed in bfloat16 or wider, within the bound.
A program may use at most 128 MiB of HBM per device.

v0:
```python
import jax
import jax.numpy as jnp
from jax import lax
from jax.sharding import PartitionSpec as P

H = 12
NNEAR = 4
NFAR = 16


def rms_norm(values, gain):
    mean_sq = jnp.mean(values * values, axis=-1, keepdims=True)
    return values * lax.rsqrt(mean_sq + 1e-05) * gain


def attend(query_block, key_values, live_blocks):
    model_width = query_block.shape[1]
    head_size = model_width // H
    keys = key_values[:, :, :model_width].reshape(-1, H, head_size)
    values = key_values[:, :, model_width:].reshape(-1, H, head_size)
    heads = query_block.reshape(-1, H, head_size)
    scores = jnp.einsum("qhd,khd->hqk", heads, keys, preferred_element_type=jnp.float32) / jnp.sqrt(
        jnp.float32(head_size)
    )
    key_live = jnp.repeat(live_blocks, key_values.shape[1])
    scores = jnp.where(key_live[None, None, :], scores, jnp.float32(-1e30))
    top = jnp.max(scores, axis=-1, keepdims=True)
    weights = jnp.exp(scores - top)
    total = jnp.sum(weights, axis=-1)
    mixed = jnp.einsum(
        "hqk,khd->qhd", weights.astype(jnp.bfloat16), values, preferred_element_type=jnp.float32
    )
    mixed = mixed / jnp.transpose(total)[:, :, None]
    return mixed.reshape(-1, model_width).astype(jnp.bfloat16)


def body(
    tokens, key_blocks, counts, norm_gain, qkv_weight, out_weight, mlp_gain, up_weight, down_weight
):
    model_width = tokens.shape[1]
    own_blocks = key_blocks.shape[0]
    block_len = tokens.shape[0] // own_blocks
    slabs_n = lax.axis_size("gz")
    slab_blocks = own_blocks * lax.axis_size("row")
    inputs = tokens.astype(jnp.float32)
    normed = rms_norm(inputs, norm_gain).astype(jnp.bfloat16)
    projected = jnp.dot(normed, qkv_weight, preferred_element_type=jnp.float32).astype(jnp.bfloat16)
    queries = projected[:, :model_width].reshape(own_blocks, block_len, model_width)
    kv_own = projected[:, model_width:].reshape(own_blocks, block_len, 2 * model_width)
    slab_kv = lax.all_gather(kv_own, "row", axis=0, tiled=True)
    owner_slab = key_blocks // slab_blocks
    within = key_blocks % slab_blocks
    slab_table = jnp.arange(slabs_n, dtype=jnp.int32)
    slab_count = jnp.sum(jnp.where(owner_slab[:, :, None] == slab_table, counts, 0), axis=-1)
    live = within < slab_count
    near_rows = within[:, :NNEAR]
    far_owner = owner_slab[:, NNEAR:].reshape(-1)
    far_local = (key_blocks[:, NNEAR:] % own_blocks).reshape(-1)
    request_count = far_owner.shape[0]
    per_owner = request_count // slabs_n
    slab_hits = (far_owner[:, None] == slab_table[None, :]).astype(jnp.int32)
    slot_rank = jnp.sum((jnp.cumsum(slab_hits, axis=0) - 1) * slab_hits, axis=1)
    far_slot = far_owner * per_owner + slot_rank
    slot_hits = far_slot[:, None] == jnp.arange(request_count, dtype=jnp.int32)[None, :]
    request = jnp.sum(jnp.where(slot_hits, far_local[:, None], 0), axis=0)
    wanted = lax.all_to_all(
        request.reshape(slabs_n, per_owner), "gz", split_axis=0, concat_axis=0, tiled=True
    ).reshape(-1)
    kv_sent = kv_own[wanted].reshape(slabs_n, per_owner, block_len, 2 * model_width)
    far_kv = lax.all_to_all(kv_sent, "gz", split_axis=0, concat_axis=0, tiled=True).reshape(
        request_count, block_len, 2 * model_width
    )
    far_slots = far_slot.reshape(own_blocks, NFAR)

    def one_block(packed):
        query_block, near_row, slot_row, live_blocks = packed
        gathered = jnp.concatenate([slab_kv[near_row], far_kv[slot_row]], axis=0)
        return attend(query_block, gathered, live_blocks)

    attended = lax.map(one_block, (queries, near_rows, far_slots, live)).reshape(-1, model_width)
    residual = (inputs + jnp.dot(attended, out_weight, preferred_element_type=jnp.float32)).astype(
        jnp.bfloat16
    )
    normed_two = rms_norm(residual.astype(jnp.float32), mlp_gain).astype(jnp.bfloat16)
    hidden = jax.nn.gelu(jnp.dot(normed_two, up_weight, preferred_element_type=jnp.float32)).astype(
        jnp.bfloat16
    )
    result = residual.astype(jnp.float32) + jnp.dot(
        hidden, down_weight, preferred_element_type=jnp.float32
    )
    return result.astype(jnp.bfloat16)


def solution(mesh):
    return jax.shard_map(
        body,
        mesh=mesh,
        in_specs=(
            P(("gz", "row"), None),
            P(("gz", "row"), None),
            P(),
            P(),
            P(),
            P(),
            P(),
            P(),
            P(),
        ),
        out_specs=P(("gz", "row"), None),
        check_vma=False,
    )
```

profile of v0, /device:TPU:34, one launch (start us, length us, event | category | flops | bytes accessed | tf_op | source)
XLA Modules:
  0.0 899.9 jit_solution(1121670228715320951)
XLA Ops:
  9.8 19.2 %all-to-all-start = ((s32[128,1,1]{2,1,0:T(1,128)}), s32[128,1,1]{2,1,0:T(1,128)S(1)}, u32[]{:S(2)}, u32[]{:S(2)}) async-start(s32[128,1,1]{2,1,0:T(1,128)} %copy.50), calls=%async_computation | async-start | bytes 131072 | tf_op jit(solution)/shard_map/all_to_all | solution.py:66
  33.1 10.2 %all-to-all-done = s32[128,1,1]{2,1,0:T(1,128)S(1)} async-done(((s32[128,1,1]{2,1,0:T(1,128)}), s32[128,1,1]{2,1,0:T(1,128)S(1)}, u32[]{:S(2)}, u32[]{:S(2)}) %all-to-all-start) | async-done | bytes 544 | tf_op jit(solution)/shard_map/all_to_all | solution.py:66
  45.6 8.3 gather_fusion.2
  53.9 7.6 all-to-all-start.1
  65.7 46.3 %all-gather.2.cloned.1.call-done = bf16[32,64,768]{2,1,0:T(8,128)(2,1)} async-done(((bf16[8,64,768]{2,1,0:T(8,128)(2,1)}), bf16[32,64,768]{2,1,0:T(8,128)(2,1)}) %all-gather.2.cloned.1.call-update) | async-done | bytes 3145744 | tf_op jit(solution)/shard_map/all_gather | solution.py:50
  112.0 496.7 %all-to-all-done.1 = bf16[128,1,64,768]{3,2,1,0:T(8,128)(2,1)} async-done(((bf16[128,1,64,768]{3,2,1,0:T(8,128)(2,1)}), bf16[128,1,64,768]{3,2,1,0:T(8,128)(2,1)}, u32[]{:S(2)}, u32[]{:S(2)}) %all-to-all-start.1) | async-done | bytes 12582944 | tf_op jit(solution)/shard_map/all_to_all | solution.py:70
  608.7 278.2 %while.10 = (s32[]{:T(128)}, bf16[8,64,384]{2,1,0:T(8,128)(2,1)}, s32[8,4]{1,0:T(8,128)}, bf16[32,64,768]{2,1,0:T(8,128)(2,1)}, s32[8,16]{1,0:T(8,128)}, /*index...) while((s32[]{:T(128)}, bf16[8,64,384]{2,1,0:T(8,128)(2,1)}, ...), condition=%wide.region_8.9_spmd, body=%wide.region_5.8_spmd.sunk | while | flops 132760128 | bytes 49673220 | solution.py:80
  613.4 5.2 gather_fusion.1
  619.9 3.0 fusion.76
  622.9 2.8 copy.69
  634.4 2.8 copy.67
  639.6 3.1 fusion.79
  648.1 5.2 gather_fusion.1
  654.7 3.0 fusion.76
  657.6 2.8 copy.69
  669.2 2.8 copy.67
  674.4 3.1 fusion.79
  682.9 5.2 gather_fusion.1
  689.4 3.0 fusion.76
  692.4 2.8 copy.69
  704.0 2.8 copy.67
  709.2 3.1 fusion.79
  717.7 5.2 gather_fusion.1
  724.2 3.0 fusion.76
  727.2 2.8 copy.69
  738.8 2.8 copy.67
  743.9 3.1 fusion.79
  752.5 5.2 gather_fusion.1
  759.0 3.0 fusion.76
  762.0 2.8 copy.69
  773.5 2.8 copy.67
  778.7 3.1 fusion.79
  787.2 5.2 gather_fusion.1
  793.8 3.0 fusion.76
  796.7 2.8 copy.69
  808.3 2.8 copy.67
  813.5 3.1 fusion.79
  822.0 5.2 gather_fusion.1
  828.5 3.0 fusion.76
  831.5 2.8 copy.69
  843.1 2.8 copy.67
  848.3 3.1 fusion.79
  856.8 5.2 gather_fusion.1
  863.3 3.0 fusion.76
  866.3 2.8 copy.69
  877.9 2.8 copy.67
  883.0 3.1 fusion.79
  888.6 3.5 fusion.29
  (197 shorter events, 158.8 us)
Async XLA Ops:
  6.5 882.0 %copy-start = (bf16[1536,384]{1,0:T(8,128)(2,1)S(1)}, bf16[1536,384]{1,0:T(8,128)(2,1)}, u32[]{:S(2)}) copy-start(bf16[1536,384]{1,0:T(8,128)(2,1)} %param.19) | copy-start | bytes 3538948
  9.8 33.5 %all-to-all-start = ((s32[128,1,1]{2,1,0:T(1,128)}), s32[128,1,1]{2,1,0:T(1,128)S(1)}, u32[]{:S(2)}, u32[]{:S(2)}) async-start(s32[128,1,1]{2,1,0:T(1,128)} %copy.50), calls=%async_computation | async-start | bytes 131072 | tf_op jit(solution)/shard_map/all_to_all | solution.py:66
  30.1 0.8 copy-start.3
  33.1 20.9 %copy-start.2 = (bf16[512,768]{1,0:T(8,128)(2,1)}, bf16[512,768]{1,0:T(8,128)(2,1)S(1)}, u32[]{:S(2)}) copy-start(bf16[512,768]{1,0:T(8,128)(2,1)S(1)} %slice.35) | copy-start | bytes 2359300
  53.9 10.0 %copy-start.4 = (s32[128]{0:T(128)S(1)}, s32[128]{0:T(128)}, u32[]{:S(2)}) copy-start(s32[128]{0:T(128)} %param.13) | copy-start | bytes 1540
  53.9 554.8 %all-to-all-start.1 = ((bf16[128,1,64,768]{3,2,1,0:T(8,128)(2,1)}), bf16[128,1,64,768]{3,2,1,0:T(8,128)(2,1)}, u32[]{:S(2)}, u32[]{:S(2)}) async-start(bf16[128,1,64,768]{3,2,1,0:T(8,128)(2,1)} %bitcast.77), calls=%async_computation.1 | async-start | bytes 25165824 | tf_op jit(solution)/shard_map/all_to_all | solution.py:70
  61.5 50.5 %all-gather.2.cloned.1.call-start = ((), (), s32[]{:S(2)}) async-start(), calls=%async_computation.2 | async-start | bytes 3932160 | tf_op jit(solution)/shard_map/all_gather | solution.py:50
  631.8 1.9 copy-start.1
  666.6 1.9 copy-start.1
  701.4 1.9 copy-start.1
  736.2 1.9 copy-start.1
  770.9 1.9 copy-start.1
  805.7 1.9 copy-start.1
  840.5 1.9 copy-start.1
  875.3 1.9 copy-start.1
Sparse Core Ops, SparseCore 0:
  64.5 47.5 all-gather.1
where the time goes:
time: 903 us; the launch traced here: 900 us
  waiting for transfers between devices  554 us (61%)
  local copies, waits for them, and re-layouts  236 us (26%)
  matrix products  48.5 us (5%)
  starting transfers between devices  27 us (3%)
  other arithmetic  21.2 us (2%)
  between operations  13.5 us (1%)
    all_to_all x1, waiting for transfers between devices, body(): lax.all_to_all(kv_sent, 'gz', split_axis=0, concat_axis=0, tiled=True)  497 us
    gather x16, local copies, waits for them, and re-layouts, one_block(): gathered = jnp.concatenate([slab_kv[near_row], far_kv[slot_row]], axis=0)  61.5 us
    all_gather x1, waiting for transfers between devices, body(): slab_kv = lax.all_gather(kv_own, 'row', axis=0, tiled=True)  46.3 us
    slice x16, local copies, waits for them, and re-layouts, attend(): keys = key_values[:, :, :model_width].reshape(-1, H, head_size)  46.1 us
    dot_general x8, matrix products, attend(): jnp.einsum('hqk,khd->qhd', weights.astype(jnp.bfloat16), values, preferre...  25.1 us
    slice x8, local copies, waits for them, and re-layouts, attend(): values = key_values[:, :, model_width:].reshape(-1, H, head_size)  22.3 us
    while x24, local copies, waits for them, and re-layouts  21.4 us
    all_to_all x1, starting transfers between devices, body(): lax.all_to_all(request.reshape(slabs_n, per_owner), 'gz', split_axis=0, c...  19.2 us
  transfers between devices with their start and end apart: 3, of which 3 were waited for; matrix products, arithmetic and copies ran while one was open for 1% of the time, Pallas kernels for 0%

commit v1 on v0

--- a/solution.py
+++ b/solution.py
@@ -6,6 +6,12 @@
 H = 12
 NNEAR = 4
 NFAR = 16
+
+
+def joined_along(pieces, dim):
+    pieces = jnp.moveaxis(pieces, 0, dim)
+    shape = pieces.shape
+    return pieces.reshape(*shape[:dim], shape[dim] * shape[dim + 1], *shape[dim + 2 :])
 
 
 def rms_norm(values, gain):
@@ -47,7 +53,19 @@
     projected = jnp.dot(normed, qkv_weight, preferred_element_type=jnp.float32).astype(jnp.bfloat16)
     queries = projected[:, :model_width].reshape(own_blocks, block_len, model_width)
     kv_own = projected[:, model_width:].reshape(own_blocks, block_len, 2 * model_width)
-    slab_kv = lax.all_gather(kv_own, "row", axis=0, tiled=True)
+    size = lax.axis_size("row")
+    pairs = [(i, (i + 1) % size) for i in range(size)]
+    back = [(b, a) for a, b in pairs]
+    lower, upper = ([], [])
+    for step in range(size - 1):
+        if step % 2 == 0:
+            lower.append(lax.ppermute(lower[-1] if lower else kv_own, "row", pairs))
+        else:
+            upper.append(lax.ppermute(upper[-1] if upper else kv_own, "row", back))
+    blocks = jnp.stack([*lower[::-1], kv_own, *upper])
+    shift = lax.axis_index("row") - len(lower)
+    blocks = blocks[(jnp.arange(size) - shift) % size]
+    slab_kv = joined_along(blocks, 0)
     owner_slab = key_blocks // slab_blocks
     within = key_blocks % slab_blocks
     slab_table = jnp.arange(slabs_n, dtype=jnp.int32)

time: 903 us -> 842 us (0.932)
  matrix products: 48.5 us -> 29.6 us
  waiting for transfers between devices: 554 us -> 537 us
  local copies, waits for them, and re-layouts: 236 us -> 220 us
  between operations: 13.5 us -> 0.19 us
    all_gather x1 -> x0, waiting for transfers between devices: 46.3 us -> none  [body(): slab_kv = lax.all_gather(kv_own, 'row', axis=0, tiled=True)]
    ppermute x0 -> x3, waiting for transfers between devices: none -> 30 us  [the longest x2 30 us: body(): lower.append(lax.ppermute(lower[-1] if lower else kv_own, 'row', pairs))]
    dot_general x8, matrix products: 25.1 us -> 5.77 us  [attend(): jnp.einsum('hqk,khd->qhd', weights.astype(jnp.bfloat16), values, preferre...]
    while x24 -> x120, local copies, waits for them, and re-layouts: 21.4 us -> 10 us
    select_n x16, other arithmetic: 10.9 us -> 0.19 us  [one_block(): gathered = jnp.concatenate([slab_kv[near_row], far_kv[slot_row]], axis=0)]
    ppermute x0 -> x3, starting transfers between devices: none -> 9.41 us  [the longest x2 6.96 us: body(): lower.append(lax.ppermute(lower[-1] if lower else kv_own, 'row', pairs))]
  transfers between devices with their start and end apart: 3 -> 5, of which waited for: 3 -> 4; matrix products, arithmetic and copies ran while one was open for 1% -> 2% of each run, Pallas kernels for 0% -> 0%
where the time goes in v1:
time: 842 us; the launch traced here: 840 us
  waiting for transfers between devices  537 us (64%)
  local copies, waits for them, and re-layouts  220 us (26%)
  starting transfers between devices  36 us (4%)
  matrix products  29.6 us (4%)
  other arithmetic  15.6 us (2%)
    all_to_all x1, waiting for transfers between devices, body(): lax.all_to_all(kv_sent, 'gz', split_axis=0, concat_axis=0, tiled=True)  497 us
    gather x16, local copies, waits for them, and re-layouts, one_block(): gathered = jnp.concatenate([slab_kv[near_row], far_kv[slot_row]], axis=0)  61.4 us
    slice x16, local copies, waits for them, and re-layouts, attend(): keys = key_values[:, :, :model_width].reshape(-1, H, head_size)  46.2 us
    ppermute x2, waiting for transfers between devices, body(): lower.append(lax.ppermute(lower[-1] if lower else kv_own, 'row', pairs))  30 us
    slice x8, local copies, waits for them, and re-layouts, attend(): values = key_values[:, :, model_width:].reshape(-1, H, head_size)  22.3 us
    all_to_all x1, starting transfers between devices, body(): lax.all_to_all(request.reshape(slabs_n, per_owner), 'gz', split_axis=0, c...  19.2 us
    reshape x8, local copies, waits for them, and re-layouts, attend(): values = key_values[:, :, model_width:].reshape(-1, H, head_size)  19 us
    reshape x8, local copies, waits for them, and re-layouts, attend(): keys = key_values[:, :, :model_width].reshape(-1, H, head_size)  18.6 us
  transfers between devices with their start and end apart: 5, of which 4 were waited for; matrix products, arithmetic and copies ran while one was open for 2% of the time, Pallas kernels for 0%

profile of v1, /device:TPU:34, one launch (start us, length us, event | category | flops | bytes accessed | tf_op | source)
XLA Modules:
  0.0 839.6 jit_solution(14190456981781282104)
XLA Ops:
  3.8 19.2 %all-to-all-start = ((s32[128,1,1]{2,1,0:T(1,128)}), s32[128,1,1]{2,1,0:T(1,128)S(1)}, u32[]{:S(2)}, u32[]{:S(2)}) async-start(s32[128,1,1]{2,1,0:T(1,128)} %copy.48), calls=%async_computation | async-start | bytes 131072 | tf_op jit(solution)/shard_map/all_to_all | solution.py:84
  27.1 10.2 %all-to-all-done = s32[128,1,1]{2,1,0:T(1,128)S(1)} async-done(((s32[128,1,1]{2,1,0:T(1,128)}), s32[128,1,1]{2,1,0:T(1,128)S(1)}, u32[]{:S(2)}, u32[]{:S(2)}) %all-to-all-start) | async-done | bytes 544 | tf_op jit(solution)/shard_map/all_to_all | solution.py:84
  39.7 8.3 gather_fusion.3
  48.0 7.5 all-to-all-start.1
  55.4 3.4 collective-permute-start
  62.2 14.8 %collective-permute-done = bf16[8,64,768]{2,1,0:T(8,128)(2,1)} collective-permute-done((bf16[8,64,768]{2,1,0:T(8,128)(2,1)S(1)}, bf16[8,64,768]{2,1,0:T(8,128)(2,1)}, u32[]{:S(2)}, u32[]{:S(2)}) %collective-permute-start) | collective-permute-done | bytes 786464 | tf_op jit(solution)/shard_map/ppermute | solution.py:62
  77.0 3.6 collective-permute-start.1
  82.8 15.1 %collective-permute-done.1 = bf16[8,64,768]{2,1,0:T(8,128)(2,1)S(1)} collective-permute-done((bf16[8,64,768]{2,1,0:T(8,128)(2,1)}, bf16[8,64,768]{2,1,0:T(8,128)(2,1)S(1)}, u32[]{:S(2)}, u32[]{:S(2)}) %collective-permute-start.1) | collective-permute-done | bytes 786464 | tf_op jit(solution)/shard_map/ppermute | solution.py:62
  97.9 3.1 pad_maximum_fusion
  101.0 4.4 gather_fusion.2
  105.4 497.3 %all-to-all-done.1 = bf16[128,1,64,768]{3,2,1,0:T(8,128)(2,1)} async-done(((bf16[128,1,64,768]{3,2,1,0:T(8,128)(2,1)}), bf16[128,1,64,768]{3,2,1,0:T(8,128)(2,1)}, u32[]{:S(2)}, u32[]{:S(2)}) %all-to-all-start.1) | async-done | bytes 12582944 | tf_op jit(solution)/shard_map/all_to_all | solution.py:88
  602.6 230.8 %while.10 = (s32[]{:T(128)}, bf16[8,64,384]{2,1,0:T(8,128)(2,1)}, s32[8,4]{1,0:T(8,128)S(1)}, bf16[32,64,768]{2,1,0:T(8,128)(2,1)}, s32[8,16]{1,0:T(8,128)S(1)},...) while((s32[]{:T(128)}, bf16[8,64,384]{2,1,0:T(8,128)(2,1)}, ...), condition=%wide.region_8.9_spmd, body=%wide.region_5.8_spmd.sunk | while | flops 132760128 | bytes 41024440 | solution.py:98
  603.6 2.5 gather_fusion
  606.9 5.2 gather_fusion.1
  613.4 3.0 fusion.78
  616.4 2.8 copy.64
  621.6 2.8 copy.66
  635.8 5.2 gather_fusion.1
  642.3 3.0 fusion.78
  645.3 2.8 copy.64
  650.5 2.8 copy.66
  661.4 2.5 gather_fusion
  664.6 5.2 gather_fusion.1
  671.2 3.0 fusion.78
  674.1 2.8 copy.64
  679.3 2.8 copy.66
  690.2 2.5 gather_fusion
  693.5 5.2 gather_fusion.1
  700.0 3.0 fusion.78
  703.0 2.8 copy.64
  708.2 2.8 copy.66
  722.3 5.2 gather_fusion.1
  728.9 3.0 fusion.78
  731.9 2.8 copy.64
  737.0 2.8 copy.66
  751.2 5.2 gather_fusion.1
  757.7 3.0 fusion.78
  760.7 2.8 copy.64
  765.9 2.8 copy.66
  780.1 5.2 gather_fusion.1
  786.6 3.0 fusion.78
  789.6 2.8 copy.64
  794.7 2.8 copy.66
  808.9 5.2 gather_fusion.1
  815.4 3.0 fusion.78
  818.4 2.8 copy.64
  823.6 2.8 copy.66
  835.1 3.5 fusion.29
  (300 shorter events, 130.4 us)
Async XLA Ops:
  0.0 835.1 %copy-start = (bf16[1536,384]{1,0:T(8,128)(2,1)S(1)}, bf16[1536,384]{1,0:T(8,128)(2,1)}, u32[]{:S(2)}) copy-start(bf16[1536,384]{1,0:T(8,128)(2,1)} %param.19) | copy-start | bytes 3538948
  3.8 33.5 %all-to-all-start = ((s32[128,1,1]{2,1,0:T(1,128)}), s32[128,1,1]{2,1,0:T(1,128)S(1)}, u32[]{:S(2)}, u32[]{:S(2)}) async-start(s32[128,1,1]{2,1,0:T(1,128)} %copy.48), calls=%async_computation | async-start | bytes 131072 | tf_op jit(solution)/shard_map/all_to_all | solution.py:84
  48.0 554.7 %all-to-all-start.1 = ((bf16[128,1,64,768]{3,2,1,0:T(8,128)(2,1)}), bf16[128,1,64,768]{3,2,1,0:T(8,128)(2,1)}, u32[]{:S(2)}, u32[]{:S(2)}) async-start(bf16[128,1,64,768]{3,2,1,0:T(8,128)(2,1)} %bitcast.84), calls=%async_computation.1 | async-start | bytes 25165824 | tf_op jit(solution)/shard_map/all_to_all | solution.py:88
  55.4 21.6 %collective-permute-start = (bf16[8,64,768]{2,1,0:T(8,128)(2,1)S(1)}, bf16[8,64,768]{2,1,0:T(8,128)(2,1)}, u32[]{:S(2)}, u32[]{:S(2)}) collective-permute-start(bf16[8,64,768]{2,1,0:T(8,128)(2,1)S(1)} %bitcast.81), channel_id=1, source_target_pairs={{0,1},{1,2},{2,3},{3,0},{4,5},{5,6},{6,7},{7,4},{8,9},{9,10},{10,1... | collective-permute-start | bytes 2359304 | tf_op jit(solution)/shard_map/ppermute | solution.py:62
  58.9 23.9 %collective-permute-start.2 = (bf16[8,64,768]{2,1,0:T(8,128)(2,1)S(1)}, bf16[8,64,768]{2,1,0:T(8,128)(2,1)}, u32[]{:S(2)}, u32[]{:S(2)}) collective-permute-start(bf16[8,64,768]{2,1,0:T(8,128)(2,1)S(1)} %bitcast.82), channel_id=1, source_target_pairs={{1,0},{2,1},{3,2},{0,3},{5,4},{6,5},{7,6},{4,7},{9,8},{10,9},{11,1... | collective-permute-start | bytes 2359304 | tf_op jit(solution)/shard_map/ppermute | solution.py:64
  77.0 20.9 %collective-permute-start.1 = (bf16[8,64,768]{2,1,0:T(8,128)(2,1)}, bf16[8,64,768]{2,1,0:T(8,128)(2,1)S(1)}, u32[]{:S(2)}, u32[]{:S(2)}) collective-permute-start(bf16[8,64,768]{2,1,0:T(8,128)(2,1)} %collective-permute-done), channel_id=1, source_target_pairs={{0,1},{1,2},{2,3},{3,0},{4,5},{5,6},{6,7},{7,4},{8,9},{9,10},{10,1... | collective-permute-start | bytes 2359304 | tf_op jit(solution)/shard_map/ppermute | solution.py:62
  602.6 232.5 %copy-start.10 = (f32[384]{0:T(512)S(1)}, f32[384]{0:T(512)}, u32[]{:S(2)}) copy-start(f32[384]{0:T(512)} %param.17) | copy-start | bytes 4612
  602.6 10.8 %copy-start.3 = (bf16[8,64,384]{2,1,0:T(8,128)(2,1)}, bf16[8,64,384]{2,1,0:T(8,128)(2,1)S(1)}, u32[]{:S(2)}) copy-start(bf16[8,64,384]{2,1,0:T(8,128)(2,1)S(1)} %get-tuple-element.200) | copy-start | bytes 1179652 | tf_op jit(solution)/shard_map/while
  602.6 10.8 %copy-start.6 = (s32[8,4]{1,0:T(8,128)}, s32[8,4]{1,0:T(8,128)S(1)}, u32[]{:S(2)}) copy-start(s32[8,4]{1,0:T(8,128)S(1)} %get-tuple-element.195) | copy-start | bytes 388 | tf_op jit(solution)/shard_map/while
  602.6 10.8 %copy-start.8 = (pred[8,20]{1,0:T(8,128)(4,1)}, pred[8,20]{1,0:T(8,128)(4,1)S(1)}, u32[]{:S(2)}) copy-start(pred[8,20]{1,0:T(8,128)(4,1)S(1)} %get-tuple-element.199) | copy-start | bytes 484 | tf_op jit(solution)/shard_map/while
  629.6 1.9 copy-start.4
  629.6 1.9 copy-start.7
  631.5 10.8 %copy-start.3 = (bf16[8,64,384]{2,1,0:T(8,128)(2,1)}, bf16[8,64,384]{2,1,0:T(8,128)(2,1)S(1)}, u32[]{:S(2)}) copy-start(bf16[8,64,384]{2,1,0:T(8,128)(2,1)S(1)} %get-tuple-element.200) | copy-start | bytes 1179652 | tf_op jit(solution)/shard_map/while
  631.5 10.8 %copy-start.6 = (s32[8,4]{1,0:T(8,128)}, s32[8,4]{1,0:T(8,128)S(1)}, u32[]{:S(2)}) copy-start(s32[8,4]{1,0:T(8,128)S(1)} %get-tuple-element.195) | copy-start | bytes 388 | tf_op jit(solution)/shard_map/while
  631.5 10.8 %copy-start.8 = (pred[8,20]{1,0:T(8,128)(4,1)}, pred[8,20]{1,0:T(8,128)(4,1)S(1)}, u32[]{:S(2)}) copy-start(pred[8,20]{1,0:T(8,128)(4,1)S(1)} %get-tuple-element.199) | copy-start | bytes 484 | tf_op jit(solution)/shard_map/while
  658.4 1.9 copy-start.4
  658.4 1.9 copy-start.7
  660.3 10.8 %copy-start.3 = (bf16[8,64,384]{2,1,0:T(8,128)(2,1)}, bf16[8,64,384]{2,1,0:T(8,128)(2,1)S(1)}, u32[]{:S(2)}) copy-start(bf16[8,64,384]{2,1,0:T(8,128)(2,1)S(1)} %get-tuple-element.200) | copy-start | bytes 1179652 | tf_op jit(solution)/shard_map/while
  660.3 10.8 %copy-start.6 = (s32[8,4]{1,0:T(8,128)}, s32[8,4]{1,0:T(8,128)S(1)}, u32[]{:S(2)}) copy-start(s32[8,4]{1,0:T(8,128)S(1)} %get-tuple-element.195) | copy-start | bytes 388 | tf_op jit(solution)/shard_map/while
  660.4 10.8 %copy-start.8 = (pred[8,20]{1,0:T(8,128)(4,1)}, pred[8,20]{1,0:T(8,128)(4,1)S(1)}, u32[]{:S(2)}) copy-start(pred[8,20]{1,0:T(8,128)(4,1)S(1)} %get-tuple-element.199) | copy-start | bytes 484 | tf_op jit(solution)/shard_map/while
  687.3 1.9 copy-start.4
  687.3 1.9 copy-start.7
  687.3 1.9 copy-start.9
  689.2 10.8 %copy-start.3 = (bf16[8,64,384]{2,1,0:T(8,128)(2,1)}, bf16[8,64,384]{2,1,0:T(8,128)(2,1)S(1)}, u32[]{:S(2)}) copy-start(bf16[8,64,384]{2,1,0:T(8,128)(2,1)S(1)} %get-tuple-element.200) | copy-start | bytes 1179652 | tf_op jit(solution)/shard_map/while
  689.2 10.8 %copy-start.6 = (s32[8,4]{1,0:T(8,128)}, s32[8,4]{1,0:T(8,128)S(1)}, u32[]{:S(2)}) copy-start(s32[8,4]{1,0:T(8,128)S(1)} %get-tuple-element.195) | copy-start | bytes 388 | tf_op jit(solution)/shard_map/while
  689.2 10.8 %copy-start.8 = (pred[8,20]{1,0:T(8,128)(4,1)}, pred[8,20]{1,0:T(8,128)(4,1)S(1)}, u32[]{:S(2)}) copy-start(pred[8,20]{1,0:T(8,128)(4,1)S(1)} %get-tuple-element.199) | copy-start | bytes 484 | tf_op jit(solution)/shard_map/while
  716.1 1.9 copy-start.4
  716.1 1.9 copy-start.7
  718.1 10.8 %copy-start.3 = (bf16[8,64,384]{2,1,0:T(8,128)(2,1)}, bf16[8,64,384]{2,1,0:T(8,128)(2,1)S(1)}, u32[]{:S(2)}) copy-start(bf16[8,64,384]{2,1,0:T(8,128)(2,1)S(1)} %get-tuple-element.200) | copy-start | bytes 1179652 | tf_op jit(solution)/shard_map/while
  718.1 10.8 %copy-start.6 = (s32[8,4]{1,0:T(8,128)}, s32[8,4]{1,0:T(8,128)S(1)}, u32[]{:S(2)}) copy-start(s32[8,4]{1,0:T(8,128)S(1)} %get-tuple-element.195) | copy-start | bytes 388 | tf_op jit(solution)/shard_map/while
  718.1 10.8 %copy-start.8 = (pred[8,20]{1,0:T(8,128)(4,1)}, pred[8,20]{1,0:T(8,128)(4,1)S(1)}, u32[]{:S(2)}) copy-start(pred[8,20]{1,0:T(8,128)(4,1)S(1)} %get-tuple-element.199) | copy-start | bytes 484 | tf_op jit(solution)/shard_map/while
  745.0 1.9 copy-start.4
  745.0 1.9 copy-start.7
  746.9 10.8 %copy-start.3 = (bf16[8,64,384]{2,1,0:T(8,128)(2,1)}, bf16[8,64,384]{2,1,0:T(8,128)(2,1)S(1)}, u32[]{:S(2)}) copy-start(bf16[8,64,384]{2,1,0:T(8,128)(2,1)S(1)} %get-tuple-element.200) | copy-start | bytes 1179652 | tf_op jit(solution)/shard_map/while
  746.9 10.8 %copy-start.6 = (s32[8,4]{1,0:T(8,128)}, s32[8,4]{1,0:T(8,128)S(1)}, u32[]{:S(2)}) copy-start(s32[8,4]{1,0:T(8,128)S(1)} %get-tuple-element.195) | copy-start | bytes 388 | tf_op jit(solution)/shard_map/while
  746.9 10.8 %copy-start.8 = (pred[8,20]{1,0:T(8,128)(4,1)}, pred[8,20]{1,0:T(8,128)(4,1)S(1)}, u32[]{:S(2)}) copy-start(pred[8,20]{1,0:T(8,128)(4,1)S(1)} %get-tuple-element.199) | copy-start | bytes 484 | tf_op jit(solution)/shard_map/while
  773.8 1.9 copy-start.4
  773.9 1.9 copy-start.7
  775.8 10.8 %copy-start.3 = (bf16[8,64,384]{2,1,0:T(8,128)(2,1)}, bf16[8,64,384]{2,1,0:T(8,128)(2,1)S(1)}, u32[]{:S(2)}) copy-start(bf16[8,64,384]{2,1,0:T(8,128)(2,1)S(1)} %get-tuple-element.200) | copy-start | bytes 1179652 | tf_op jit(solution)/shard_map/while
  775.8 10.8 %copy-start.6 = (s32[8,4]{1,0:T(8,128)}, s32[8,4]{1,0:T(8,128)S(1)}, u32[]{:S(2)}) copy-start(s32[8,4]{1,0:T(8,128)S(1)} %get-tuple-element.195) | copy-start | bytes 388 | tf_op jit(solution)/shard_map/while
  775.8 10.8 %copy-start.8 = (pred[8,20]{1,0:T(8,128)(4,1)}, pred[8,20]{1,0:T(8,128)(4,1)S(1)}, u32[]{:S(2)}) copy-start(pred[8,20]{1,0:T(8,128)(4,1)S(1)} %get-tuple-element.199) | copy-start | bytes 484 | tf_op jit(solution)/shard_map/while
  802.7 1.9 copy-start.4
  802.7 1.9 copy-start.7
  804.6 10.8 %copy-start.3 = (bf16[8,64,384]{2,1,0:T(8,128)(2,1)}, bf16[8,64,384]{2,1,0:T(8,128)(2,1)S(1)}, u32[]{:S(2)}) copy-start(bf16[8,64,384]{2,1,0:T(8,128)(2,1)S(1)} %get-tuple-element.200) | copy-start | bytes 1179652 | tf_op jit(solution)/shard_map/while
  804.6 10.8 %copy-start.6 = (s32[8,4]{1,0:T(8,128)}, s32[8,4]{1,0:T(8,128)S(1)}, u32[]{:S(2)}) copy-start(s32[8,4]{1,0:T(8,128)S(1)} %get-tuple-element.195) | copy-start | bytes 388 | tf_op jit(solution)/shard_map/while
  804.6 10.8 %copy-start.8 = (pred[8,20]{1,0:T(8,128)(4,1)}, pred[8,20]{1,0:T(8,128)(4,1)S(1)}, u32[]{:S(2)}) copy-start(pred[8,20]{1,0:T(8,128)(4,1)S(1)} %get-tuple-element.199) | copy-start | bytes 484 | tf_op jit(solution)/shard_map/while
  831.6 1.9 copy-start.4
  831.6 1.9 copy-start.7
  (17 other events, 24.6 us)
